TPU v7x, 128 devices: a whole 4x4x4 slice. The times are simulated.
128 devices in a mesh: cell: 64 (over x, y, z), gpt: 2 (over core).
Axes of the slice: x: 4, y: 4, z: 4, core: 2. Of those that a mesh axis runs over, the one named last changes fastest.
Arguments:
- fields: bfloat16 [6, 16, 524288], P(None, None, 'cell'), may hold values from 0.00099 to 0.1002, as said below
- surface: bfloat16 [2, 524288], P(None, 'cell'), may hold values from 0.19921875 to 0.94921875
- sunlit: int32 [524288], P('cell'), may hold values from 0 to 1
- routing: int32 [4096], P('cell'), may hold values from -1 to 63, as said below
- stencil: int32 [7, 524288], P(None, 'cell'), may hold values from -128 to 128
- weights: float32 [7, 524288], P(None, 'cell'), may hold values from 0.1 to 1
- optics: float32 [3, 112], P(None, 'gpt'), may hold values from 0.05 to 20
- solar_flux: float32 [112], P('gpt'), may hold values from 0.5 to 2
Outputs:
- heating_rate: float32 [16, 524288], P('gpt', 'cell')
Inputs may be any that keep to these rules, and one draw needn't show every extreme that they name: `routing`: each device is named by exactly 32 blocks in all, and by at most 1 of the 64 blocks of any one device. All fields are positive.
All inputs are finite; a program needn't handle non-finite values.
Results may differ from a plain program's by a relative error of at most 0.0003.
Values may be sent and summed in bfloat16 or wider, within the bound.
No kernel may reach another device: no remote copies, remote signals or barrier semaphores. Data moves between devices by JAX's collectives and lax.ppermute only.
A program may use at most 64 MiB of HBM per device.

v0:
```python
import jax
import jax.numpy as jnp
from jax import lax
from jax.sharding import PartitionSpec as P

G = 112
BLK = 128
HW = 128


def with_halo(block, sides, width):
    for axis, dim in sides:
        count = lax.axis_size(axis)
        forward = [(i, i + 1) for i in range(count - 1)]
        forward.append((count - 1, 0))
        backward = [(target, source) for source, target in forward]
        low = lax.ppermute(
            lax.slice_in_dim(block, block.shape[dim] - width, None, axis=dim), axis, forward
        )
        high = lax.ppermute(lax.slice_in_dim(block, 0, width, axis=dim), axis, backward)
        block = jnp.concatenate([low, block, high], axis=dim)
    return block


def column_heat(fields, geometry, optics, solar_flux, factor):
    levels = fields.shape[1]
    cosine = geometry[0].astype(jnp.float32)[None, :]
    albedo = geometry[1].astype(jnp.float32)[None, :]
    lit_part = geometry[2].astype(jnp.float32)[None, :]
    k_vapor = optics[0][:, None]
    k_ozone = optics[1][:, None]
    k_rayleigh = optics[2][:, None]
    incoming = solar_flux[:, None] * lit_part * cosine
    optical_depth = jnp.zeros_like(incoming)
    scattering = []
    absorbed = []
    direct = []
    for layer_index in range(levels):
        column = fields[:, layer_index].astype(jnp.float32)
        clouds = column[3] + column[4]
        scatter_now = k_rayleigh * column[0] + 0.9 * clouds + 0.8 * column[5]
        absorb_now = k_vapor * column[1] + k_ozone * column[2] + 0.1 * clouds + 0.2 * column[5]
        optical_depth = optical_depth + scatter_now + absorb_now
        scattering.append(scatter_now)
        absorbed.append(absorb_now)
        direct.append(incoming * jnp.exp(-optical_depth / cosine))
    coupling = [0.5 * (scattering[i] + scattering[i + 1]) + 0.1 for i in range(levels - 1)]
    ratios = []
    partial_sol = []
    for layer_index in range(levels):
        above = coupling[layer_index - 1] if layer_index > 0 else 0.5
        below = coupling[layer_index] if layer_index < levels - 1 else 0.5
        diagonal = absorbed[layer_index] + above + below
        source = scattering[layer_index] * direct[layer_index]
        if layer_index == levels - 1:
            source = source + albedo * direct[layer_index]
        if layer_index > 0:
            pivots = diagonal - above * ratios[layer_index - 1]
            solved = (source + above * partial_sol[layer_index - 1]) / pivots
        else:
            pivots = diagonal
            solved = source / pivots
        ratios.append(below / pivots)
        partial_sol.append(solved)
    diffuse = partial_sol[levels - 1]
    heat_rows = [None] * levels
    for layer_index in reversed(range(levels)):
        if layer_index < levels - 1:
            diffuse = partial_sol[layer_index] + ratios[layer_index] * diffuse
        heat_rows[layer_index] = (
            jnp.sum(absorbed[layer_index] * (diffuse + direct[layer_index]), axis=0) * factor
        )
    return jnp.stack(heat_rows)


def solve_columns(fields, geometry, optics, solar_flux, factor):
    levels = fields.shape[1]
    columns = fields.shape[2]
    width = min(columns, 8 * BLK)

    def one_group(group_index, heat):
        start = group_index * width
        part_fields = lax.dynamic_slice_in_dim(fields, start, width, 2)
        part_geometry = lax.dynamic_slice_in_dim(geometry, start, width, 1)
        group_heat = column_heat(part_fields, part_geometry, optics, solar_flux, factor)
        return lax.dynamic_update_slice_in_dim(heat, group_heat, start, 1)

    return lax.fori_loop(0, columns // width, one_group, jnp.zeros((levels, columns), jnp.float32))


def pick_blocks(source, chosen):
    source_count = source.shape[-2]
    selector = (chosen[:, None] == jnp.arange(source_count, dtype=jnp.int32)[None, :]).astype(
        source.dtype
    )
    if source.dtype == jnp.float32:
        picked = jnp.einsum(
            "...sk,os->...ok",
            source,
            selector,
            preferred_element_type=jnp.float32,
            precision=lax.Precision.HIGHEST,
        )
    else:
        picked = jnp.einsum("...sk,os->...ok", source, selector, preferred_element_type=jnp.float32)
    return picked.astype(source.dtype)


def reduce_bands(heating):
    summed = lax.psum(heating, "gpt")
    each_rows = heating.shape[0] // lax.axis_size("gpt")
    return lax.dynamic_slice_in_dim(summed, lax.axis_index("gpt") * each_rows, each_rows, 0)


def interpolate(extended, stencil, weights, own_columns):
    block_count = own_columns // BLK
    row_count = extended.shape[0]
    windows = jnp.concatenate(
        [
            extended[:, 0:own_columns].reshape(row_count, block_count, BLK),
            extended[:, BLK : BLK + own_columns].reshape(row_count, block_count, BLK),
            extended[:, 2 * BLK : 2 * BLK + own_columns].reshape(row_count, block_count, BLK),
        ],
        axis=2,
    )
    normalized = weights / jnp.sum(weights, axis=0, keepdims=True)
    window_pos = jnp.arange(3 * BLK, dtype=jnp.int32)[None, :, None]
    inner_pos = jnp.arange(BLK, dtype=jnp.int32)[None, None, :]
    mixing = jnp.zeros((block_count, 3 * BLK, BLK), jnp.float32)
    for stencil_point in range(stencil.shape[0]):
        target = inner_pos + HW + stencil[stencil_point].reshape(block_count, 1, BLK)
        share = normalized[stencil_point].reshape(block_count, 1, BLK)
        mixing = mixing + jnp.where(window_pos == target, share, 0.0)
    result = jnp.einsum(
        "rnw,nwk->rnk",
        windows,
        mixing,
        preferred_element_type=jnp.float32,
        precision=lax.Precision.HIGHEST,
    )
    return result.reshape(row_count, own_columns)


def local(fields, surface, sunlit, routing, stencil, weights, optics, solar_flux):
    block_count = routing.shape[0]
    own_columns = fields.shape[2]
    levels = fields.shape[1]
    factor = 1.0 / G
    routed_blocks = (routing >= 0).astype(jnp.int32)
    lit_columns = (sunlit.reshape(block_count, BLK) * routed_blocks[:, None]).reshape(own_columns)
    geometry = jnp.stack([surface[0], surface[1], lit_columns.astype(jnp.bfloat16)])
    cell_count = lax.axis_size("cell")
    own_index = lax.axis_index("cell")
    capacity = block_count // cell_count
    slot_total = cell_count * capacity
    reduced_count = block_count // 2
    block_ids = jnp.arange(block_count, dtype=jnp.int32)
    earlier = (routing[None, :] == routing[:, None]) & (block_ids[None, :] < block_ids[:, None])
    prior_count = jnp.sum(earlier.astype(jnp.int32), axis=1)
    slot_of_block = jnp.where(routing >= 0, routing * capacity + prior_count, -1)
    slot_rows = jnp.arange(slot_total, dtype=jnp.int32)
    matches = slot_of_block[None, :] == slot_rows[:, None]
    source_block = jnp.sum(jnp.where(matches, block_ids[None, :], 0), axis=1)
    blocks = fields.reshape(6, levels, block_count, BLK)
    geometry_blocks = geometry.reshape(3, 1, block_count, BLK)
    send_fields = pick_blocks(blocks, source_block)
    send_geometry = pick_blocks(geometry_blocks, source_block)
    recv_fields, recv_geometry = (
        lax.all_to_all(send_fields, "cell", split_axis=2, concat_axis=2, tiled=True),
        lax.all_to_all(send_geometry, "cell", split_axis=2, concat_axis=2, tiled=True),
    )
    all_routes = lax.all_gather(routing, "cell", axis=0, tiled=True)
    incoming = jnp.sum(
        (all_routes.reshape(cell_count, block_count) == own_index).astype(jnp.int32), axis=1
    )
    source_of_slot = slot_rows // capacity
    copy_index = slot_rows % capacity
    slot_live = copy_index < jnp.take(incoming, source_of_slot)
    live_int = slot_live.astype(jnp.int32)
    compact_rank = jnp.cumsum(live_int) - live_int
    reduced_ids = jnp.arange(reduced_count, dtype=jnp.int32)
    picked = (compact_rank[None, :] == reduced_ids[:, None]) & slot_live[None, :]
    picked_slot = jnp.sum(jnp.where(picked, slot_rows[None, :], 0), axis=1)
    reduced_fields = pick_blocks(recv_fields, picked_slot).reshape(6, levels, reduced_count * BLK)
    reduced_geometry = pick_blocks(recv_geometry, picked_slot).reshape(3, reduced_count * BLK)
    heating = solve_columns(reduced_fields, reduced_geometry, optics, solar_flux, factor)
    own_levels = reduce_bands(heating)
    half_levels = own_levels.shape[0]
    back_index = jnp.where(slot_live, compact_rank, 0)
    returned = pick_blocks(own_levels.reshape(half_levels, reduced_count, BLK), back_index)
    arrived = lax.all_to_all(returned, "cell", split_axis=1, concat_axis=1, tiled=True)
    home_heat = pick_blocks(arrived, slot_of_block)
    dynamics = home_heat.reshape(half_levels, own_columns)
    extended = with_halo(dynamics, (("cell", 1),), HW)
    return interpolate(extended, stencil, weights, own_columns)


def solution(mesh):
    placed = (
        P(None, None, "cell"),
        P(None, "cell"),
        P("cell"),
        P("cell"),
        P(None, "cell"),
        P(None, "cell"),
        P(None, "gpt"),
        P("gpt"),
    )
    return jax.shard_map(
        local, mesh=mesh, in_specs=placed, out_specs=P("gpt", "cell"), check_vma=False
    )
```

profile of v0, /device:TPU:0, one launch (start us, length us, event | category | flops | bytes accessed | tf_op | source)
XLA Modules:
  0.0 547.9 jit_solution(16854829055907314181)
XLA Ops:
  11.4 11.5 %all-to-all-start.1 = ((bf16[3,1,64,128]{3,0,1,2:T(4,128)(2,1)}), bf16[3,1,64,128]{3,0,1,2:T(4,128)(2,1)S(1)}, u32[]{:S(2)}, u32[]{:S(2)}) async-start(bf16[3,1,64,128]{3,0,1,2:T(4,128)(2,1)} %copy.24), calls=%async_computation.1 | async-start | bytes 131072 | tf_op jit(solution)/shard_map/all_to_all | solution.py:170
  22.9 1.3 dynamic-slice
  25.8 349.3 %all-reduce = s32[4096]{0:T(1024)S(1)} all-reduce(s32[4096]{0:T(1024)S(1)} %dynamic-update-slice), channel_id=1, replica_groups=mesh['cell'=64,'gpt'=2] {'cell'}, use_global_device_ids=true, to_apply=%add | all-reduce | flops 4096 | bytes 32768
  376.5 1.8 copy.31
  379.1 2.2 copy.22
  381.3 4.7 all-to-all-start
  386.4 16.9 %all-to-all-done = bf16[6,16,64,128]{3,1,0,2:T(8,128)(2,1)S(1)} async-done(((bf16[6,16,64,128]{3,1,0,2:T(8,128)(2,1)}), bf16[6,16,64,128]{3,1,0,2:T(8,128)(2,1)S(1)}, u32[]{:S(2)}, u32[]{:S(2)}) %all-to-all-start) | async-done | bytes 1572896 | tf_op jit(solution)/shard_map/all_to_all | solution.py:169
  404.2 63.0 %while.13 = (s32[]{:T(128)}, f32[16,4096]{1,0:T(8,128)S(1)}, f32[3,56]{1,0:T(4,128)S(1)}, bf16[6,16,4096]{2,1,0:T(8,128)(2,1)S(1)}, f32[56]{0:T(128)S(1)}, /*ind...) while((s32[]{:T(128)}, f32[16,4096]{1,0:T(8,128)S(1)}, ...), condition=%wide.region_23.24_spmd, body=%wide.region_6.23_spmd.sunk | while | flops 70601744 | bytes 23048272 | solution.py:88
  405.8 5.0 multiply_reduce_fusion.30
  415.2 1.3 multiply_reduce_fusion.40
  416.5 1.3 multiply_reduce_fusion.36
  421.4 5.0 multiply_reduce_fusion.30
  430.8 1.3 multiply_reduce_fusion.40
  432.1 1.3 multiply_reduce_fusion.36
  437.0 5.0 multiply_reduce_fusion.30
  447.7 1.3 multiply_reduce_fusion.36
  452.7 5.0 multiply_reduce_fusion.30
  463.3 1.3 multiply_reduce_fusion.36
  468.2 19.4 %all-reduce.3.cloned.1.call-done = f32[16,4096]{1,0:T(8,128)} async-done(((f32[16,4096]{1,0:T(8,128)}), f32[16,4096]{1,0:T(8,128)}) %all-reduce.3.cloned.1.call-update) | async-done | bytes 262160 | tf_op jit(solution)/shard_map/psum | solution.py:110
  489.7 10.4 %all-to-all-start.2 = ((f32[8,64,128]{2,0,1:T(8,128)}), f32[8,64,128]{2,0,1:T(8,128)S(1)}, u32[]{:S(2)}, u32[]{:S(2)}) async-start(f32[8,64,128]{2,0,1:T(8,128)} %copy.26), calls=%async_computation.2 | async-start | bytes 524288 | tf_op jit(solution)/shard_map/all_to_all | solution.py:191
  500.3 10.7 %all-to-all-done.2 = f32[8,64,128]{2,0,1:T(8,128)S(1)} async-done(((f32[8,64,128]{2,0,1:T(8,128)}), f32[8,64,128]{2,0,1:T(8,128)S(1)}, u32[]{:S(2)}, u32[]{:S(2)}) %all-to-all-start.2) | async-done | bytes 262176 | tf_op jit(solution)/shard_map/all_to_all | solution.py:191
  512.1 6.9 %collective-permute-start.1 = (f32[8,128]{1,0:T(8,128)S(1)}, f32[8,128]{1,0:T(8,128)S(1)}, u32[]{:S(2)}, u32[]{:S(2)}) collective-permute-start(f32[8,128]{1,0:T(8,128)S(1)} %get-tuple-element.394), channel_id=1, source_target_pairs={{2,0},{4,2},{6,4},{8,6},{10,8},{12,10},{14,12},{16,14},{18,16},{20... | collective-permute-start | bytes 12296 | tf_op jit(solution)/shard_map/ppermute | solution.py:20
  519.0 1.6 collective-permute-done
  520.8 20.1 %fusion.46 = f32[8,8192]{1,0:T(8,128)} fusion(f32[64,128]{1,0:T(8,128)S(1)} %bitcast.965, s32[64,128]{1,0:T(8,128)S(1)} %get-tuple-element.417, f32[64,128]{1,0:T(8,128)S(1)} %bitcast.966, s32[64,128]{1,0:T(8,128)S(1)} %get-tuple-element.416, f32[64,128]{1,0:T(8,128)S(1)} %bitcast.967, s32[64,128]{1,0:T(8,128)S(1)} %get-tuple-element.415, ...), kind=kOutput, calls=%fused_computation.298 | convolution fusion | flops 364904448 | bytes 1507328 | tf_op jit(solution)/shard_map/rnw,nwk->rnk/dot_general | solution.py:134
  (285 shorter events, 46.7 us)
Async XLA Ops:
  11.4 370.0 %all-to-all-start.1 = ((bf16[3,1,64,128]{3,0,1,2:T(4,128)(2,1)}), bf16[3,1,64,128]{3,0,1,2:T(4,128)(2,1)S(1)}, u32[]{:S(2)}, u32[]{:S(2)}) async-start(bf16[3,1,64,128]{3,0,1,2:T(4,128)(2,1)} %copy.24), calls=%async_computation.1 | async-start | bytes 131072 | tf_op jit(solution)/shard_map/all_to_all | solution.py:170
  379.1 2.2 copy-start.1
  381.3 21.9 %all-to-all-start = ((bf16[6,16,64,128]{3,1,0,2:T(8,128)(2,1)}), bf16[6,16,64,128]{3,1,0,2:T(8,128)(2,1)S(1)}, u32[]{:S(2)}, u32[]{:S(2)}) async-start(bf16[6,16,64,128]{3,1,0,2:T(8,128)(2,1)} %copy.22), calls=%async_computation | async-start | bytes 3145728 | tf_op jit(solution)/shard_map/all_to_all | solution.py:169
  386.0 101.6 %all-reduce.3.cloned.1.call-start = ((), (), s32[]{:S(2)}) async-start(), calls=%async_computation.3 | async-start | bytes 524288 | tf_op jit(solution)/shard_map/psum | solution.py:110
  386.3 17.9 %copy-start = (f32[56]{0:T(128)S(1)}, f32[56]{0:T(128)}, u32[]{:S(2)}) copy-start(f32[56]{0:T(128)} %param.17) | copy-start | bytes 676
  386.4 17.9 %copy-start.4 = (f32[3,56]{1,0:T(4,128)S(1)}, f32[3,56]{1,0:T(4,128)}, u32[]{:S(2)}) copy-start(f32[3,56]{1,0:T(4,128)} %param.16) | copy-start | bytes 2020
  404.2 63.8 %copy-start.3 = (s32[7,8192]{1,0:T(8,128)S(1)}, s32[7,8192]{1,0:T(8,128)}, u32[]{:S(2)}) copy-start(s32[7,8192]{1,0:T(8,128)} %param.14) | copy-start | bytes 688132
  467.3 0.7 copy-start.2
  489.7 21.2 %all-to-all-start.2 = ((f32[8,64,128]{2,0,1:T(8,128)}), f32[8,64,128]{2,0,1:T(8,128)S(1)}, u32[]{:S(2)}, u32[]{:S(2)}) async-start(f32[8,64,128]{2,0,1:T(8,128)} %copy.26), calls=%async_computation.2 | async-start | bytes 524288 | tf_op jit(solution)/shard_map/all_to_all | solution.py:191
  511.4 9.1 %collective-permute-start = (f32[8,128]{1,0:T(8,128)S(1)}, f32[8,128]{1,0:T(8,128)S(1)}, u32[]{:S(2)}, u32[]{:S(2)}) collective-permute-start(f32[8,128]{1,0:T(8,128)S(1)} %get-tuple-element.393), channel_id=1, source_target_pairs={{0,2},{2,4},{4,6},{6,8},{8,10},{10,12},{12,14},{14,16},{16,18},{18... | collective-permute-start | bytes 12296 | tf_op jit(solution)/shard_map/ppermute | solution.py:17
  512.1 8.5 %collective-permute-start.1 = (f32[8,128]{1,0:T(8,128)S(1)}, f32[8,128]{1,0:T(8,128)S(1)}, u32[]{:S(2)}, u32[]{:S(2)}) collective-permute-start(f32[8,128]{1,0:T(8,128)S(1)} %get-tuple-element.394), channel_id=1, source_target_pairs={{2,0},{4,2},{6,4},{8,6},{10,8},{12,10},{14,12},{16,14},{18,16},{20... | collective-permute-start | bytes 12296 | tf_op jit(solution)/shard_map/ppermute | solution.py:20
Sparse Core Ops, SparseCore 0:
  468.2 19.3 all-reduce.2
where the time goes:
time: 553 us; the launch traced here: 548 us
  blocking collectives  349 us (63%)
  other arithmetic  64.2 us (12%)
  waiting for transfers between devices  48.5 us (9%)
  starting transfers between devices  34.2 us (6%)
  matrix products  22.3 us (4%)
  between operations  14.6 us (3%)
  local copies, waits for them, and re-layouts  12.6 us (2%)
    unnamed x1, blocking collectives  349 us
    reduce_sum x56, other arithmetic, column_heat(): jnp.sum(absorbed[layer_index] * (diffuse + direct[layer_index]), axis=0)  55.5 us
    dot_general x1, matrix products, interpolate(): jnp.einsum('rnw,nwk->rnk', windows, mixing, preferred_element_type=jnp.fl...  20.1 us
    psum x1, waiting for transfers between devices, reduce_bands(): summed = lax.psum(heating, 'gpt')  19.4 us
    all_to_all x1, waiting for transfers between devices, local(): lax.all_to_all(send_fields, 'cell', split_axis=2, concat_axis=2, tiled=True)  16.9 us
    all_to_all x1, starting transfers between devices, local(): lax.all_to_all(send_geometry, 'cell', split_axis=2, concat_axis=2, tiled=...  11.5 us
  transfers between devices with their start and end apart: 6, of which 4 were waited for; matrix products, arithmetic and copies ran while one was open for 2% of the time, Pallas kernels for 0%

commit v1 on v0

--- a/solution.py
+++ b/solution.py
@@ -107,7 +107,7 @@
 
 
 def reduce_bands(heating):
-    summed = lax.psum(heating, "gpt")
+    summed = jnp.sum(lax.all_gather(heating, "gpt"), axis=0)
     each_rows = heating.shape[0] // lax.axis_size("gpt")
     return lax.dynamic_slice_in_dim(summed, lax.axis_index("gpt") * each_rows, each_rows, 0)
 

time: 553 us -> 516 us (0.933)
  waiting for transfers between devices: 48.5 us -> 29.2 us
  between operations: 14.6 us -> 1.18 us
  starting transfers between devices: 34.2 us -> 28.5 us
    psum x1 -> x0, waiting for transfers between devices: 19.4 us -> none  [reduce_bands(): summed = lax.psum(heating, 'gpt')]
    all_to_all x1, starting transfers between devices: 10.4 us -> 4.63 us  [local(): lax.all_to_all(returned, 'cell', split_axis=1, concat_axis=1, tiled=True)]
  transfers between devices with their start and end apart: 6 -> 5, of which waited for: 4 -> 3; matrix products, arithmetic and copies ran while one was open for 2% -> 2% of each run, Pallas kernels for 0% -> 0%
where the time goes in v1:
time: 516 us; the launch traced here: 510 us
  blocking collectives  352 us (68%)
  other arithmetic  64.2 us (12%)
  waiting for transfers between devices  29.2 us (6%)
  starting transfers between devices  28.5 us (6%)
  matrix products  22.3 us (4%)
  local copies, waits for them, and re-layouts  11.3 us (2%)
    unnamed x1, blocking collectives  349 us
    reduce_sum x56, other arithmetic, column_heat(): jnp.sum(absorbed[layer_index] * (diffuse + direct[layer_index]), axis=0)  55.5 us
    dot_general x1, matrix products, interpolate(): jnp.einsum('rnw,nwk->rnk', windows, mixing, preferred_element_type=jnp.fl...  20.1 us
    all_to_all x1, waiting for transfers between devices, local(): lax.all_to_all(send_fields, 'cell', split_axis=2, concat_axis=2, tiled=True)  16.8 us
    all_to_all x1, starting transfers between devices, local(): lax.all_to_all(send_geometry, 'cell', split_axis=2, concat_axis=2, tiled=...  11.5 us
    all_to_all x1, waiting for transfers between devices, local(): lax.all_to_all(returned, 'cell', split_axis=1, concat_axis=1, tiled=True)  10.8 us
  transfers between devices with their start and end apart: 5, of which 3 were waited for; matrix products, arithmetic and copies ran while one was open for 2% of the time, Pallas kernels for 0%

profile of v1, /device:TPU:0, one launch (start us, length us, event | category | flops | bytes accessed | tf_op | source)
XLA Modules:
  0.0 510.4 jit_solution(15732824629089534210)
XLA Ops:
  4.8 11.5 %all-to-all-start.1 = ((bf16[3,1,64,128]{3,0,1,2:T(4,128)(2,1)}), bf16[3,1,64,128]{3,0,1,2:T(4,128)(2,1)S(1)}, u32[]{:S(2)}, u32[]{:S(2)}) async-start(bf16[3,1,64,128]{3,0,1,2:T(4,128)(2,1)} %copy.24), calls=%async_computation.1 | async-start | bytes 131072 | tf_op jit(solution)/shard_map/all_to_all | solution.py:170
  16.4 1.3 dynamic-slice
  19.3 349.4 %all-reduce = s32[4096]{0:T(1024)S(1)} all-reduce(s32[4096]{0:T(1024)S(1)} %dynamic-update-slice), channel_id=1, replica_groups=mesh['cell'=64,'gpt'=2] {'cell'}, use_global_device_ids=true, to_apply=%add | all-reduce | flops 4096 | bytes 32768
  370.0 1.8 copy.31
  373.0 2.2 copy.22
  375.2 4.8 all-to-all-start
  380.4 16.8 %all-to-all-done = bf16[6,16,64,128]{3,1,0,2:T(8,128)(2,1)S(1)} async-done(((bf16[6,16,64,128]{3,1,0,2:T(8,128)(2,1)}), bf16[6,16,64,128]{3,1,0,2:T(8,128)(2,1)S(1)}, u32[]{:S(2)}, u32[]{:S(2)}) %all-to-all-start) | async-done | bytes 1572896 | tf_op jit(solution)/shard_map/all_to_all | solution.py:169
  398.2 63.0 %while.13 = (s32[]{:T(128)}, f32[16,4096]{1,0:T(8,128)S(1)}, f32[3,56]{1,0:T(4,128)S(1)}, bf16[6,16,4096]{2,1,0:T(8,128)(2,1)S(1)}, f32[56]{0:T(128)S(1)}, /*ind...) while((s32[]{:T(128)}, f32[16,4096]{1,0:T(8,128)S(1)}, ...), condition=%wide.region_23.24_spmd, body=%wide.region_6.23_spmd.sunk | while | flops 70601744 | bytes 23048272 | solution.py:88
  399.8 5.0 multiply_reduce_fusion.30
  409.2 1.3 multiply_reduce_fusion.40
  410.5 1.3 multiply_reduce_fusion.36
  415.4 5.0 multiply_reduce_fusion.30
  424.8 1.3 multiply_reduce_fusion.40
  426.1 1.3 multiply_reduce_fusion.36
  431.0 5.0 multiply_reduce_fusion.30
  441.7 1.3 multiply_reduce_fusion.36
  446.6 5.0 multiply_reduce_fusion.30
  457.3 1.3 multiply_reduce_fusion.36
  461.3 2.2 all-gather
  464.7 4.6 all-to-all-start.2
  469.5 10.8 %all-to-all-done.2 = f32[8,64,128]{2,0,1:T(8,128)S(1)} async-done(((f32[8,64,128]{2,0,1:T(8,128)}), f32[8,64,128]{2,0,1:T(8,128)S(1)}, u32[]{:S(2)}, u32[]{:S(2)}) %all-to-all-start.2) | async-done | bytes 262176 | tf_op jit(solution)/shard_map/all_to_all | solution.py:191
  481.5 6.9 %collective-permute-start.1 = (f32[8,128]{1,0:T(8,128)S(1)}, f32[8,128]{1,0:T(8,128)S(1)}, u32[]{:S(2)}, u32[]{:S(2)}) collective-permute-start(f32[8,128]{1,0:T(8,128)S(1)} %get-tuple-element.394), channel_id=1, source_target_pairs={{2,0},{4,2},{6,4},{8,6},{10,8},{12,10},{14,12},{16,14},{18,16},{20... | collective-permute-start | bytes 12296 | tf_op jit(solution)/shard_map/ppermute | solution.py:20
  488.4 1.6 collective-permute-done
  490.1 20.1 %fusion.46 = f32[8,8192]{1,0:T(8,128)} fusion(f32[64,128]{1,0:T(8,128)S(1)} %bitcast.967, s32[64,128]{1,0:T(8,128)S(1)} %get-tuple-element.417, f32[64,128]{1,0:T(8,128)S(1)} %bitcast.968, s32[64,128]{1,0:T(8,128)S(1)} %get-tuple-element.416, f32[64,128]{1,0:T(8,128)S(1)} %bitcast.969, s32[64,128]{1,0:T(8,128)S(1)} %get-tuple-element.415, ...), kind=kOutput, calls=%fused_computation.298 | convolution fusion | flops 364904448 | bytes 1507328 | tf_op jit(solution)/shard_map/rnw,nwk->rnk/dot_general | solution.py:134
  (282 shorter events, 45.4 us)
Async XLA Ops:
  4.8 370.4 %all-to-all-start.1 = ((bf16[3,1,64,128]{3,0,1,2:T(4,128)(2,1)}), bf16[3,1,64,128]{3,0,1,2:T(4,128)(2,1)S(1)}, u32[]{:S(2)}, u32[]{:S(2)}) async-start(bf16[3,1,64,128]{3,0,1,2:T(4,128)(2,1)} %copy.24), calls=%async_computation.1 | async-start | bytes 131072 | tf_op jit(solution)/shard_map/all_to_all | solution.py:170
  371.8 1.0 copy-start.1
  375.2 4.8 copy-start.2
  375.2 22.0 %all-to-all-start = ((bf16[6,16,64,128]{3,1,0,2:T(8,128)(2,1)}), bf16[6,16,64,128]{3,1,0,2:T(8,128)(2,1)S(1)}, u32[]{:S(2)}, u32[]{:S(2)}) async-start(bf16[6,16,64,128]{3,1,0,2:T(8,128)(2,1)} %copy.22), calls=%async_computation | async-start | bytes 3145728 | tf_op jit(solution)/shard_map/all_to_all | solution.py:169
  380.4 17.8 %copy-start = (f32[56]{0:T(128)S(1)}, f32[56]{0:T(128)}, u32[]{:S(2)}) copy-start(f32[56]{0:T(128)} %param.17) | copy-start | bytes 676
  380.4 17.8 %copy-start.3 = (f32[3,56]{1,0:T(4,128)S(1)}, f32[3,56]{1,0:T(4,128)}, u32[]{:S(2)}) copy-start(f32[3,56]{1,0:T(4,128)} %param.16) | copy-start | bytes 2020
  464.7 15.6 %all-to-all-start.2 = ((f32[8,64,128]{2,0,1:T(8,128)}), f32[8,64,128]{2,0,1:T(8,128)S(1)}, u32[]{:S(2)}, u32[]{:S(2)}) async-start(f32[8,64,128]{2,0,1:T(8,128)} %copy.26), calls=%async_computation.2 | async-start | bytes 524288 | tf_op jit(solution)/shard_map/all_to_all | solution.py:191
  480.8 9.1 %collective-permute-start = (f32[8,128]{1,0:T(8,128)S(1)}, f32[8,128]{1,0:T(8,128)S(1)}, u32[]{:S(2)}, u32[]{:S(2)}) collective-permute-start(f32[8,128]{1,0:T(8,128)S(1)} %get-tuple-element.393), channel_id=1, source_target_pairs={{0,2},{2,4},{4,6},{6,8},{8,10},{10,12},{12,14},{14,16},{16,18},{18... | collective-permute-start | bytes 12296 | tf_op jit(solution)/shard_map/ppermute | solution.py:17
  481.5 8.5 %collective-permute-start.1 = (f32[8,128]{1,0:T(8,128)S(1)}, f32[8,128]{1,0:T(8,128)S(1)}, u32[]{:S(2)}, u32[]{:S(2)}) collective-permute-start(f32[8,128]{1,0:T(8,128)S(1)} %get-tuple-element.394), channel_id=1, source_target_pairs={{2,0},{4,2},{6,4},{8,6},{10,8},{12,10},{14,12},{16,14},{18,16},{20... | collective-permute-start | bytes 12296 | tf_op jit(solution)/shard_map/ppermute | solution.py:20
